TPU v7x, 128 devices: a whole 4x4x4 slice. The times are simulated.
128 devices in a mesh: seg: 32 (over y, z_hi, x), los: 4 (over z_lo, core).
Axes of the slice: x: 4, y: 4, z: 4 (z_hi: 2, z_lo: 2; z = z_hi * 2 + z_lo), core: 2. Of those that a mesh axis runs over, the one named last changes fastest.
Arguments:
- baryon_contrast: float32 [32, 128, 8192], P('seg', None, 'los'), may hold values from 0.13 to 22.2, as said below
- warmth_over_ten_thousand: float32 [32, 128, 8192], P('seg', None, 'los'), may hold values from 0.3 to 3
- peculiar_motion_shift: float32 [32, 128, 8192], P('seg', None, 'los'), may hold values from -384 to 384
- semi_extent_samples: int32 [32, 128], P(None, 'los'), may hold values from 256 to 512
- subvolume_device_lookup: int32 [32], replicated, may hold values from 0 to 31, each once
Outputs:
- flux: float32 [32, 128, 8192], P(None, 'los', 'seg')
Inputs may be any that keep to these rules, and one draw needn't show every extreme that they name: `subvolume_device_lookup`: every number once. `baryon_contrast`: positive.
All inputs are finite; a program needn't handle non-finite values.
Results may differ from a plain program's by a relative error of at most 0.0003.
Values sent between devices are 32-bit elements; how exact they have to be, the bound alone decides.
A program may use at most 64 MiB of HBM per device.

v0:
```python
import functools

import jax
import jax.numpy as jnp
from jax import lax
from jax.experimental import pallas as pl
from jax.experimental.pallas import tpu as pltpu
from jax.sharding import PartitionSpec as P

LOG2E = 1.4426950408889634
ROWS = 128
LENGTH = 2048
GROUPS = ROWS // 8
REACH = 512
SEGS, LOSS = 32, 4
WIDE = 256
CELLS = 33554432.0
MESH = pl.DeviceIdType.MESH
F32 = jnp.float32


def swap_blocks(arrays, lane):
    arrays = [list(a) for a in arrays]
    for i in range(4):
        sh = 8 << i
        bit = (lane & sh) != 0
        for m in range(16):
            if m & (1 << i):
                continue
            for v in arrays:
                a, b = v[m], v[m | (1 << i)]
                v[m] = jnp.where(bit, pltpu.roll(b, sh, 1), a)
                v[m | (1 << i)] = jnp.where(bit, b, pltpu.roll(a, 128 - sh, 1))
    return arrays


def band_kernel(perm, reach, d_ref, t_ref, v_ref, tau_ref, right_ref, left_ref, buf, W, C, NB, Q, M, Zb, S, E):
    lane = lax.broadcasted_iota(jnp.int32, (8, 128), 1)
    sub = lax.broadcasted_iota(jnp.int32, (8, 128), 0)
    gin = (lane & 7) * 16 + (lane >> 3)
    gout = (lane & 15) * 8 + (lane >> 4)
    first = lane == 0
    last = lane == 127
    zero = jnp.zeros((8, 128), F32)

    def prep(g, _):
        for i in range(8):
            y = perm[g * 8 + i]
            buf[0, pl.ds(i, 1), :] = d_ref[pl.ds(y, 1), :]
            buf[1, pl.ds(i, 1), :] = t_ref[pl.ds(y, 1), :]
            buf[2, pl.ds(i, 1), :] = v_ref[pl.ds(y, 1), :]
        dd, tt, vv = swap_blocks(
            [
                [jnp.take_along_axis(buf[n, :, m * 128 : (m + 1) * 128], gin, axis=1) for m in range(16)]
                for n in range(3)
            ],
            lane,
        )
        for t in range(16):
            C[g * 16 + t] = vv[t] + float(t)
            nb = (-LOG2E / 169.0) / tt[t]
            NB[g * 16 + t] = nb
            Q[g * 16 + t] = jnp.exp2(nb + nb)
            W[g * 16 + t] = ((0.3 / 13.0) * jnp.exp2(-1.2 * jnp.log2(tt[t]))) * (dd[t] * dd[t])
        return 0

    lax.fori_loop(0, GROUPS, prep, 0)

    zf = jnp.full((8, 128), (perm[0] >> 16).astype(F32))

    def group(g, _):
        hv = zero
        for i in range(8):
            hv = jnp.where(sub == i, reach[g * 8 + i].astype(F32), hv)
        kout = lax.div(reach[g * 8 + 7] + 15, 16)
        kin = lax.div(reach[g * 8] - 15, 16)

        def chain(ci, sign, count):
            shift = 1 if sign > 0 else 127
            hit = first if sign > 0 else last
            base = (g * 2 + ci) * 16
            for r in range(16):
                S[base + r] = zero
                E[base + r] = zero
                Zb[1, r] = zero

            def shift_up(dst):
                for r in range(16):
                    a = base + r
                    zr = pltpu.roll(S[a] + Zb[1 - dst, r], shift, 1)
                    er = pltpu.roll(E[a], shift, 1)
                    S[a] = jnp.where(hit, 0.0, zr)
                    E[a] = jnp.where(hit, zr, er)

            def cells(Z, kf, masked):
                gate = None
                for s in range(16):
                    if s % 2 == 0:
                        kb = kf if gate is None else kf + gate * zf
                    nb = NB[g * 16 + s]
                    x = kb - C[g * 16 + s]
                    m = nb * x
                    A = W[g * 16 + s] * jnp.exp2(m * x)
                    m2 = m + m
                    R = jnp.exp2(m2 + nb)
                    U = jnp.exp2(nb - m2)
                    q = Q[g * 16 + s]

                    def add(r, G):
                        term = G * M[r - s + 15] if masked else G
                        Z[r] = term if Z[r] is None else Z[r] + term

                    add(8, A)
                    G = H = A
                    for i in range(1, 9):
                        H = H * U
                        add(8 - i, H)
                        if i < 8:
                            G = G * R
                            add(8 + i, G)
                        if i < 7:
                            R = R * q
                        if i < 8:
                            U = U * q
                    gate = A

            def body(masked, n, _):
                k = kout - n
                dst = n & 1
                if masked:
                    hk = hv - (16 * k).astype(F32)
                    for i in range(31):
                        M[i] = jnp.where(hk >= float(sign * (i - 15)), 1.0, 0.0)
                Z = [None] * 16
                shift_up(dst)
                cells(Z, (sign * 16 * k + 8).astype(F32), masked)
                for r in range(16):
                    Zb[dst, r] = Z[r]
                return 0

            nm = kout - kin
            lax.fori_loop(0, nm, functools.partial(body, True), 0)
            lax.fori_loop(nm, count, functools.partial(body, False), 0)
            fin = (count - 1) & 1
            for r in range(16):
                S[base + r] = S[base + r] + Zb[fin, r]

        chain(0, 1, kout + 1)
        chain(1, -1, kout)
        return 0

    lax.fori_loop(0, GROUPS, group, 0)

    def out(g, _):
        b0 = g * 32
        b1 = b0 + 16
        tau, edge = [], []
        for r in range(16):
            zr = pltpu.roll(S[b1 + r], 127, 1)
            el = jnp.where(last, zr, pltpu.roll(E[b1 + r], 127, 1))
            tau.append(S[b0 + r] + jnp.where(last, 0.0, zr))
            edge.append(jnp.where(lane < 64, E[b0 + r], el))
        tau, edge = swap_blocks([tau, edge], lane)
        for m in range(16):
            buf[0, :, m * 128 : (m + 1) * 128] = jnp.take_along_axis(tau[m], gout, axis=1)
            if m < 4 or m >= 12:
                buf[1, :, m * 128 : (m + 1) * 128] = jnp.take_along_axis(edge[m], gout, axis=1)
        for i in range(8):
            y = perm[g * 8 + i]
            tau_ref[pl.ds(y, 1), :] = buf[0, pl.ds(i, 1), :]
            right_ref[pl.ds(y, 1), :] = buf[1, pl.ds(i, 1), 0:REACH]
            left_ref[pl.ds(y, 1), :] = buf[1, pl.ds(i, 1), LENGTH - REACH : LENGTH]
        return 0

    lax.fori_loop(0, GROUPS, out, 0)


def band_depth(perm, reach, d, t, v):
    whole = pl.BlockSpec((ROWS, LENGTH), lambda i, *_: (0, 0))
    side = pl.BlockSpec((ROWS, REACH), lambda i, *_: (0, 0))
    table = pltpu.VMEM((GROUPS * 16, 8, 128), F32)
    sums = pltpu.VMEM((GROUPS * 32, 8, 128), F32)
    return pl.pallas_call(
        band_kernel,
        out_shape=(
            jax.ShapeDtypeStruct((ROWS, LENGTH), F32),
            jax.ShapeDtypeStruct((ROWS, REACH), F32),
            jax.ShapeDtypeStruct((ROWS, REACH), F32),
        ),
        grid_spec=pltpu.PrefetchScalarGridSpec(
            num_scalar_prefetch=2,
            grid=(1,),
            in_specs=[whole] * 3,
            out_specs=[whole, side, side],
            scratch_shapes=[
                pltpu.VMEM((3, 8, LENGTH), F32),
                table,
                table,
                table,
                table,
                pltpu.VMEM((31, 8, 128), F32),
                pltpu.VMEM((2, 16, 8, 128), F32),
                sums,
                sums,
            ],
        ),
        compiler_params=pltpu.CompilerParams(vmem_limit_bytes=50 << 20),
        name="band",
    )(perm, reach, d, t, v)


def share_kernel(tau, right, left, got, sums_out, from_left, from_right, flux, relay, part, parts, local_sum, sums,
                 edge_send, edge_recv, a_send, a_recv, b_send, b_recv, p_send, p_recv, q_send, q_recv):
    seg, los = lax.axis_index("seg"), lax.axis_index("los")
    y, zh, x = lax.div(seg, 8), lax.rem(lax.div(seg, 4), 2), lax.rem(seg, 4)
    zl, core = lax.div(los, 2), lax.rem(los, 2)
    after, before = lax.rem(los + 1, LOSS), lax.rem(los + LOSS - 1, LOSS)
    me = zh * 4 + los

    def column(d):
        h = 1 - zh if d & 4 else zh
        l = (1 - zl if d & 2 else zl) * 2 + (1 - core if d & 1 else core)
        return h, l

    def plane(dy, dx):
        return lax.rem(y + dy, 4) * 8 + zh * 4 + lax.rem(x + dx, 4)

    barrier = pltpu.get_barrier_semaphore()

    def signal(s, l):
        pl.semaphore_signal(barrier, inc=1, device_id=(s, l), device_id_type=MESH)

    for d in range(1, 8):
        h, l = column(d)
        signal(y * 8 + h * 4 + x, l)
    for i in range(1, 16):
        signal(plane(i // 4, i % 4), los)
    pl.semaphore_wait(barrier, 22)

    def remote(src, dst, send, recv, s, l):
        return pltpu.make_async_remote_copy(
            src_ref=src, dst_ref=dst, send_sem=send, recv_sem=recv, device_id=(s, l), device_id_type=MESH
        )

    edges = [
        remote(right, from_left, edge_send.at[0], edge_recv.at[0], seg, after),
        remote(left, from_right, edge_send.at[1], edge_recv.at[1], seg, before),
    ]
    for copy in edges:
        copy.start()
    for copy in edges:
        copy.wait_recv()

    def rows_of(i, total):
        rows = pl.ds(pl.multiple_of(i * 8, 8), 8)
        for m in range(16):
            cols = pl.ds(m * 128, 128)
            depth = tau[rows, cols]
            if m < 4:
                depth = depth + from_left[rows, cols]
            if m >= 12:
                depth = depth + from_right[rows, pl.ds((m - 12) * 128, 128)]
            value = jnp.exp(-depth)
            flux[rows, cols] = value
            total = total + value
        return total

    part[...] = lax.fori_loop(0, GROUPS, rows_of, jnp.zeros((8, 128), F32))

    def a_part(d):
        h, l = column(d)
        return flux.at[pl.ds(pl.multiple_of(l * 32, 32), 32), pl.ds(pl.multiple_of(h * 1024, 1024), 1024)]

    def a_copy(d):
        h, l = column(d)
        return remote(a_part(d), relay.at[me], a_send.at[d], a_recv.at[me], y * 8 + h * 4 + x, l)

    def a_arrival(d):
        h, l = column(d)
        return remote(a_part(d), relay.at[h * 4 + l], a_send.at[d], a_recv.at[h * 4 + l], y * 8 + h * 4 + x, l)

    def p_copy(d):
        h, l = column(d)
        return remote(part, parts.at[d - 1], p_send.at[d - 1], p_recv.at[d - 1], y * 8 + h * 4 + x, l)

    for d in range(1, 8):
        p_copy(d).start()
    keep = pltpu.make_async_copy(a_part(0), relay.at[me], a_recv.at[me])
    for d in (4, 2, 6, 5, 3, 7, 1):
        a_copy(d).start()
    keep.start()

    total = part[...]
    for d in range(1, 8):
        p_copy(d).wait_recv()
        total = total + parts[d - 1]
    local_sum[...] = total

    def q_copy(i):
        return remote(local_sum, sums.at[i - 1], q_send.at[i - 1], q_recv.at[i - 1], plane(i // 4, i % 4), los)

    for i in range(1, 16):
        q_copy(i).start()

    def b_part(d, j):
        h, l = column(d)
        to = lax.rem(x + j, 4)
        return relay.at[h * 4 + l, :, pl.ds(pl.multiple_of(to * WIDE, WIDE), WIDE)]

    def b_copy(d, j):
        h, l = column(d)
        slot = y * 8 + h * 4 + x
        return remote(b_part(d, j), got.at[slot], b_send.at[d, j], b_recv.at[slot],
                      l * 8 + zh * 4 + lax.rem(x + j, 4), los)

    def b_keep(d):
        h, l = column(d)
        slot = y * 8 + h * 4 + x
        return pltpu.make_async_copy(b_part(d, 0), got.at[slot], b_recv.at[slot])

    def stays(d):
        return column(d)[1] == y

    def leaves(d):
        return column(d)[1] != y

    for d in (0, 1, 2, 6, 3, 7, 4, 5):
        if d == 0:
            keep.wait()
        else:
            a_arrival(d).wait_recv()
        for j in (2, 1, 3):
            b_copy(d, j).start()

        @pl.when(leaves(d))
        def _():
            b_copy(d, 0).start()

        @pl.when(stays(d))
        def _():
            b_keep(d).start()

    for i in range(1, 16):
        q_copy(i).wait_recv()
        total = total + sums[i - 1]
    sums_out[...] = total

    def take(s, _):
        ys, xs = lax.div(s, 8), lax.rem(s, 4)
        here = jnp.logical_and(ys == y, xs == x)

        @pl.when(jnp.logical_not(here))
        def _():
            remote(relay.at[0, :, pl.ds(0, WIDE)], got.at[s], b_send.at[0, 1], b_recv.at[s],
                   ys * 8 + zh * 4 + xs, los).wait_recv()

        @pl.when(here)
        def _():
            pltpu.make_async_copy(relay.at[0, :, pl.ds(0, WIDE)], got.at[s], b_recv.at[s]).wait()
        return 0

    lax.fori_loop(0, SEGS, take, 0)

    for copy in edges:
        copy.wait_send()
    for d in range(1, 8):
        a_copy(d).wait_send()
        p_copy(d).wait_send()
    for i in range(1, 16):
        q_copy(i).wait_send()
    for d in range(8):
        for j in (1, 2, 3):
            b_copy(d, j).wait_send()

        @pl.when(leaves(d))
        def _():
            b_copy(d, 0).wait_send()


def share(tau, right, left):
    vmem = pl.BlockSpec(memory_space=pltpu.VMEM)
    dma = pltpu.SemaphoreType.DMA
    return pl.pallas_call(
        share_kernel,
        out_shape=(jax.ShapeDtypeStruct((SEGS, 32, WIDE), F32), jax.ShapeDtypeStruct((8, 128), F32)),
        in_specs=[vmem] * 3,
        out_specs=(pl.BlockSpec(memory_space=pl.ANY), vmem),
        scratch_shapes=[
            pltpu.VMEM((ROWS, REACH), F32),
            pltpu.VMEM((ROWS, REACH), F32),
            pltpu.VMEM((ROWS, LENGTH), F32),
            pltpu.VMEM((8, 32, 1024), F32),
            pltpu.VMEM((8, 128), F32),
            pltpu.VMEM((7, 8, 128), F32),
            pltpu.VMEM((8, 128), F32),
            pltpu.VMEM((15, 8, 128), F32),
            dma((2,)),
            dma((2,)),
            dma((8,)),
            dma((8,)),
            dma((8, 4)),
            dma((SEGS,)),
            dma((7,)),
            dma((7,)),
            dma((15,)),
            dma((15,)),
        ],
        compiler_params=pltpu.CompilerParams(collective_id=0, has_side_effects=True, vmem_limit_bytes=24 << 20),
        name="share",
    )(tau, right, left)


def per_device(contrast, warmth, velocity, semi_extent, lookup):
    seg = lax.axis_index("seg")
    mine = lookup == seg
    own = jnp.sum(jnp.where(mine[:, None], semi_extent, 0).astype(F32), axis=0)
    h = lax.all_gather(own, "los", tiled=True)
    at = jnp.arange(ROWS)
    below = (h[None, :] < h[:, None]) | ((h[None, :] == h[:, None]) & (at[None, :] < at[:, None]))
    rank = jnp.sum(below.astype(jnp.int32), axis=1)
    hot = rank[:, None] == at[None, :]
    perm = jnp.sum(jnp.where(hot, at[:, None], 0), axis=0).astype(jnp.int32)
    reach = jnp.sum(jnp.where(hot, h[:, None], 0.0), axis=0).astype(jnp.int32)
    shape = (ROWS, LENGTH)
    tau, right, left = band_depth(
        perm, reach, contrast.reshape(shape), warmth.reshape(shape), velocity.reshape(shape)
    )
    got, sums = share(tau, right, left)
    scale = CELLS / jnp.sum(sums)
    return jnp.take(got, lookup, axis=0) * scale


def solution(mesh):
    return jax.shard_map(
        per_device,
        mesh=mesh,
        in_specs=(P("seg", None, "los"), P("seg", None, "los"), P("seg", None, "los"), P(None, "los"), P()),
        out_specs=P(None, "los", "seg"),
        check_vma=False,
    )
```

profile of v0, /device:TPU:1, one launch (start us, length us, event | category | flops | bytes accessed | tf_op | source)
XLA Modules:
  0.0 199.7 jit_solution(21138417656740406)
XLA Ops:
  0.0 0.0 copy-start.2
  0.0 0.7 copy-done.2
  0.7 0.8 convert_reduce_fusion.1
  1.5 0.0 copy-start.3
  1.5 0.6 copy-done.3
  2.1 0.6 dynamic-slice
  3.4 0.2 dynamic-update-slice
  3.6 6.8 %all-reduce = f32[128]{0:T(128)S(1)} all-reduce(f32[128]{0:T(128)S(1)} %dynamic-update-slice), channel_id=1, replica_groups=mesh['seg'=32,'los'=4] {'los'}, use_global_device_ids=true, to_apply=%add | all-reduce | flops 128 | bytes 1024
  10.4 0.2 convert_reduce_fusion
  10.6 0.1 select_reduce_fusion
  10.7 0.1 select_reduce_fusion.1.perm
  10.8 0.0 copy-start
  10.8 1.2 copy-done
  12.0 0.0 copy-start.1
  12.0 1.2 copy-done.1
  13.3 143.9 %band.1 = (f32[128,2048]{1,0:T(8,128)S(1)}, f32[128,512]{1,0:T(8,128)S(1)}, f32[128,512]{1,0:T(8,128)S(1)}) custom-call(s32[128]{0:T(128)S(1)} %select_reduce_fusion.1.perm, s32[128]{0:T(128)S(1)} %convert_element_type.11.reach, f32[128,2048]{1,0:T(8,128)S(1)} %bitcast.4, f32[128,2048]{1,0:T(8,128)S(1)} %bitcast.5, f32[128,2048]{1,0:T(8,128)} %bitcast.6), custom_call_target="tpu_custom_call" | custom-call | tf_op jit(solution)/shard_map/band/pallas_call | solution.py:183
  157.1 39.5 %share.1 = (f32[32,32,256]{2,1,0:T(8,128)S(1)}, f32[8,128]{1,0:T(8,128)S(1)}) custom-call(f32[128,2048]{1,0:T(8,128)S(1)} %get-tuple-element.10.tau, f32[128,512]{1,0:T(8,128)S(1)} %get-tuple-element.11.right, f32[128,512]{1,0:T(8,128)S(1)} %get-tuple-element.12.left), custom_call_target="tpu_custom_call" | custom-call | tf_op jit(solution)/shard_map/share/pallas_call | solution.py:383
  196.6 0.6 gather_fusion
  197.3 0.6 reduce_sum.49
  198.5 1.1 select_multiply_fusion
  (5 shorter events, 0.0 us)
Async XLA Ops:
  0.0 0.7 copy-start.2
  1.5 0.7 copy-start.3
  10.8 1.2 copy-start
  12.0 1.2 copy-start.1
where the time goes:
time: 200 us
  Pallas kernels  183 us (92%)
  blocking collectives  6.77 us (3%)
  local copies, waits for them, and re-layouts  5.19 us (3%)
  other arithmetic  2.94 us (1%)
    pallas_call x1, Pallas kernels, band_depth(): pl.pallas_call(band_kernel, out_shape=(jax.ShapeDtypeStruct((ROWS, LENGTH...  144 us
    pallas_call x1, Pallas kernels, share(): pl.pallas_call(share_kernel, out_shape=(jax.ShapeDtypeStruct((SEGS, 32, W...  39.5 us
    unnamed x1, blocking collectives  6.77 us
    unnamed x11, local copies, waits for them, and re-layouts  4.57 us

commit v1 on v0

--- a/solution.py
+++ b/solution.py
@@ -19,54 +19,37 @@
 F32 = jnp.float32
 
 
-def swap_blocks(arrays, lane):
-    arrays = [list(a) for a in arrays]
-    for i in range(4):
-        sh = 8 << i
-        bit = (lane & sh) != 0
-        for m in range(16):
-            if m & (1 << i):
-                continue
-            for v in arrays:
-                a, b = v[m], v[m | (1 << i)]
-                v[m] = jnp.where(bit, pltpu.roll(b, sh, 1), a)
-                v[m | (1 << i)] = jnp.where(bit, b, pltpu.roll(a, 128 - sh, 1))
-    return arrays
-
-
-def band_kernel(perm, reach, d_ref, t_ref, v_ref, tau_ref, right_ref, left_ref, buf, W, C, NB, Q, M, Zb, S, E):
+def band_kernel(perm, reach, d_ref, t_ref, v_ref, tau_ref, edge_ref, W, C, NB, Q, M, Zb, S, E):
     lane = lax.broadcasted_iota(jnp.int32, (8, 128), 1)
     sub = lax.broadcasted_iota(jnp.int32, (8, 128), 0)
-    gin = (lane & 7) * 16 + (lane >> 3)
-    gout = (lane & 15) * 8 + (lane >> 4)
-    first = lane == 0
-    last = lane == 127
     zero = jnp.zeros((8, 128), F32)
 
-    def prep(g, _):
+    def gather(g, _):
+        at = pl.ds(pl.multiple_of(g * 16, 16), 16)
         for i in range(8):
             y = perm[g * 8 + i]
-            buf[0, pl.ds(i, 1), :] = d_ref[pl.ds(y, 1), :]
-            buf[1, pl.ds(i, 1), :] = t_ref[pl.ds(y, 1), :]
-            buf[2, pl.ds(i, 1), :] = v_ref[pl.ds(y, 1), :]
-        dd, tt, vv = swap_blocks(
-            [
-                [jnp.take_along_axis(buf[n, :, m * 128 : (m + 1) * 128], gin, axis=1) for m in range(16)]
-                for n in range(3)
-            ],
-            lane,
-        )
+            W[at, i : i + 1, :] = d_ref[:, pl.ds(y, 1), :]
+            NB[at, i : i + 1, :] = t_ref[:, pl.ds(y, 1), :]
+            C[at, i : i + 1, :] = v_ref[:, pl.ds(y, 1), :]
+        return 0
+
+    lax.fori_loop(0, GROUPS, gather, 0)
+
+    def prep(g, _):
         for t in range(16):
-            C[g * 16 + t] = vv[t] + float(t)
-            nb = (-LOG2E / 169.0) / tt[t]
-            NB[g * 16 + t] = nb
-            Q[g * 16 + t] = jnp.exp2(nb + nb)
-            W[g * 16 + t] = ((0.3 / 13.0) * jnp.exp2(-1.2 * jnp.log2(tt[t]))) * (dd[t] * dd[t])
+            a = g * 16 + t
+            warmth = NB[a]
+            contrast = W[a]
+            nb = (-LOG2E / 169.0) / warmth
+            C[a] = C[a] + float(t)
+            NB[a] = nb
+            Q[a] = jnp.exp2(nb + nb)
+            W[a] = ((0.3 / 13.0) * jnp.exp2(-1.2 * jnp.log2(warmth))) * (contrast * contrast)
+            S[a] = zero
+            E[a] = zero
         return 0
 
     lax.fori_loop(0, GROUPS, prep, 0)
-
-    zf = jnp.full((8, 128), (perm[0] >> 16).astype(F32))
 
     def group(g, _):
         hv = zero
@@ -74,137 +57,94 @@
             hv = jnp.where(sub == i, reach[g * 8 + i].astype(F32), hv)
         kout = lax.div(reach[g * 8 + 7] + 15, 16)
         kin = lax.div(reach[g * 8] - 15, 16)
-
-        def chain(ci, sign, count):
-            shift = 1 if sign > 0 else 127
-            hit = first if sign > 0 else last
-            base = (g * 2 + ci) * 16
+        base = g * 16
+        for r in range(16):
+            Zb[1, r] = zero
+
+        def place(dst, sk):
+            shift = lax.rem(sk + 128, 128)
+            inside = jnp.logical_and(lane >= sk, lane < sk + 128)
             for r in range(16):
-                S[base + r] = zero
-                E[base + r] = zero
-                Zb[1, r] = zero
-
-            def shift_up(dst):
-                for r in range(16):
-                    a = base + r
-                    zr = pltpu.roll(S[a] + Zb[1 - dst, r], shift, 1)
-                    er = pltpu.roll(E[a], shift, 1)
-                    S[a] = jnp.where(hit, 0.0, zr)
-                    E[a] = jnp.where(hit, zr, er)
-
-            def cells(Z, kf, masked):
-                gate = None
-                for s in range(16):
-                    if s % 2 == 0:
-                        kb = kf if gate is None else kf + gate * zf
-                    nb = NB[g * 16 + s]
-                    x = kb - C[g * 16 + s]
-                    m = nb * x
-                    A = W[g * 16 + s] * jnp.exp2(m * x)
-                    m2 = m + m
-                    R = jnp.exp2(m2 + nb)
-                    U = jnp.exp2(nb - m2)
-                    q = Q[g * 16 + s]
-
-                    def add(r, G):
-                        term = G * M[r - s + 15] if masked else G
-                        Z[r] = term if Z[r] is None else Z[r] + term
-
-                    add(8, A)
-                    G = H = A
-                    for i in range(1, 9):
-                        H = H * U
-                        add(8 - i, H)
-                        if i < 8:
-                            G = G * R
-                            add(8 + i, G)
-                        if i < 7:
-                            R = R * q
-                        if i < 8:
-                            U = U * q
-                    gate = A
-
-            def body(masked, n, _):
-                k = kout - n
-                dst = n & 1
-                if masked:
-                    hk = hv - (16 * k).astype(F32)
-                    for i in range(31):
-                        M[i] = jnp.where(hk >= float(sign * (i - 15)), 1.0, 0.0)
-                Z = [None] * 16
-                shift_up(dst)
-                cells(Z, (sign * 16 * k + 8).astype(F32), masked)
-                for r in range(16):
-                    Zb[dst, r] = Z[r]
-                return 0
-
-            nm = kout - kin
-            lax.fori_loop(0, nm, functools.partial(body, True), 0)
-            lax.fori_loop(nm, count, functools.partial(body, False), 0)
-            fin = (count - 1) & 1
+                z = pltpu.roll(Zb[1 - dst, r], shift, 1)
+                S[base + r] = S[base + r] + jnp.where(inside, z, 0.0)
+                E[base + r] = E[base + r] + jnp.where(inside, 0.0, z)
+
+        def cells(Z, kf, masked):
+            for s in range(16):
+                nb = NB[base + s]
+                x = kf - C[base + s]
+                m = nb * x
+                A = W[base + s] * jnp.exp2(m * x)
+                m2 = m + m
+                R = jnp.exp2(m2 + nb)
+                U = jnp.exp2(nb - m2)
+                q = Q[base + s]
+
+                def add(r, G):
+                    term = G * M[r - s + 15] if masked else G
+                    Z[r] = term if Z[r] is None else Z[r] + term
+
+                add(8, A)
+                G = H = A
+                for i in range(1, 9):
+                    H = H * U
+                    add(8 - i, H)
+                    if i < 8:
+                        G = G * R
+                        add(8 + i, G)
+                    if i < 7:
+                        R = R * q
+                    if i < 8:
+                        U = U * q
+
+        def body(side, where, n, carry):
+            before, dst = carry
+            sk = where(n)
+            if side:
+                hk = hv - (16 * side * sk).astype(F32)
+                for i in range(31):
+                    M[i] = jnp.where(hk >= float(side * (i - 15)), 1.0, 0.0)
+            Z = [None] * 16
+            place(dst, before)
+            cells(Z, (16 * sk + 8).astype(F32), side)
             for r in range(16):
-                S[base + r] = S[base + r] + Zb[fin, r]
-
-        chain(0, 1, kout + 1)
-        chain(1, -1, kout)
+                Zb[dst, r] = Z[r]
+            return sk, 1 - dst
+
+        carry = (jnp.int32(0), jnp.int32(0))
+        carry = lax.fori_loop(0, kout - kin, functools.partial(body, -1, lambda n: n - kout), carry)
+        carry = lax.fori_loop(0, kout - kin, functools.partial(body, 1, lambda n: kout - n), carry)
+        carry = lax.fori_loop(
+            0, 2 * kin + 1, functools.partial(body, 0, lambda n: jnp.where(n < kin, n - kin, 2 * kin - n)), carry
+        )
+        fin = 1 - carry[1]
+        for r in range(16):
+            S[base + r] = S[base + r] + Zb[fin, r]
         return 0
 
     lax.fori_loop(0, GROUPS, group, 0)
 
-    def out(g, _):
-        b0 = g * 32
-        b1 = b0 + 16
-        tau, edge = [], []
-        for r in range(16):
-            zr = pltpu.roll(S[b1 + r], 127, 1)
-            el = jnp.where(last, zr, pltpu.roll(E[b1 + r], 127, 1))
-            tau.append(S[b0 + r] + jnp.where(last, 0.0, zr))
-            edge.append(jnp.where(lane < 64, E[b0 + r], el))
-        tau, edge = swap_blocks([tau, edge], lane)
-        for m in range(16):
-            buf[0, :, m * 128 : (m + 1) * 128] = jnp.take_along_axis(tau[m], gout, axis=1)
-            if m < 4 or m >= 12:
-                buf[1, :, m * 128 : (m + 1) * 128] = jnp.take_along_axis(edge[m], gout, axis=1)
+    def scatter(g, _):
+        at = pl.ds(pl.multiple_of(g * 16, 16), 16)
         for i in range(8):
             y = perm[g * 8 + i]
-            tau_ref[pl.ds(y, 1), :] = buf[0, pl.ds(i, 1), :]
-            right_ref[pl.ds(y, 1), :] = buf[1, pl.ds(i, 1), 0:REACH]
-            left_ref[pl.ds(y, 1), :] = buf[1, pl.ds(i, 1), LENGTH - REACH : LENGTH]
-        return 0
-
-    lax.fori_loop(0, GROUPS, out, 0)
-
+            tau_ref[:, pl.ds(y, 1), :] = S[at, i : i + 1, :]
+            edge_ref[:, pl.ds(y, 1), :] = E[at, i : i + 1, :]
+        return 0
+
+    lax.fori_loop(0, GROUPS, scatter, 0)
 
 def band_depth(perm, reach, d, t, v):
-    whole = pl.BlockSpec((ROWS, LENGTH), lambda i, *_: (0, 0))
-    side = pl.BlockSpec((ROWS, REACH), lambda i, *_: (0, 0))
+    whole = pl.BlockSpec((16, ROWS, 128), lambda i, *_: (0, 0, 0))
     table = pltpu.VMEM((GROUPS * 16, 8, 128), F32)
-    sums = pltpu.VMEM((GROUPS * 32, 8, 128), F32)
     return pl.pallas_call(
         band_kernel,
-        out_shape=(
-            jax.ShapeDtypeStruct((ROWS, LENGTH), F32),
-            jax.ShapeDtypeStruct((ROWS, REACH), F32),
-            jax.ShapeDtypeStruct((ROWS, REACH), F32),
+        out_shape=(jax.ShapeDtypeStruct((16, ROWS, 128), F32),) * 2,
+        grid_spec=pltpu.PrefetchScalarGridSpec(
+            num_scalar_prefetch=2, grid=(1,), in_specs=[whole] * 3, out_specs=[whole] * 2,
+            scratch_shapes=[table] * 4 + [pltpu.VMEM((31, 8, 128), F32), pltpu.VMEM((2, 16, 8, 128), F32), table, table],
         ),
-        grid_spec=pltpu.PrefetchScalarGridSpec(
-            num_scalar_prefetch=2,
-            grid=(1,),
-            in_specs=[whole] * 3,
-            out_specs=[whole, side, side],
-            scratch_shapes=[
-                pltpu.VMEM((3, 8, LENGTH), F32),
-                table,
-                table,
-                table,
-                table,
-                pltpu.VMEM((31, 8, 128), F32),
-                pltpu.VMEM((2, 16, 8, 128), F32),
-                sums,
-                sums,
-            ],
-        ),
-        compiler_params=pltpu.CompilerParams(vmem_limit_bytes=50 << 20),
+        compiler_params=pltpu.CompilerParams(vmem_limit_bytes=40 << 20),
         name="band",
     )(perm, reach, d, t, v)
 
@@ -421,11 +361,15 @@
     hot = rank[:, None] == at[None, :]
     perm = jnp.sum(jnp.where(hot, at[:, None], 0), axis=0).astype(jnp.int32)
     reach = jnp.sum(jnp.where(hot, h[:, None], 0.0), axis=0).astype(jnp.int32)
-    shape = (ROWS, LENGTH)
-    tau, right, left = band_depth(
-        perm, reach, contrast.reshape(shape), warmth.reshape(shape), velocity.reshape(shape)
-    )
-    got, sums = share(tau, right, left)
+
+    def by_lane(a):
+        return a.reshape(ROWS, 128, 16).transpose(2, 0, 1)
+
+    def in_order(a):
+        return a.transpose(1, 2, 0).reshape(ROWS, -1)
+
+    tau, edge = band_depth(perm, reach, by_lane(contrast), by_lane(warmth), by_lane(velocity))
+    got, sums = share(in_order(tau), in_order(edge[:, :, :32]), in_order(edge[:, :, 96:]))
     scale = CELLS / jnp.sum(sums)
     return jnp.take(got, lookup, axis=0) * scale
 

time: 200 us -> 185 us (0.925)
  Pallas kernels: 183 us -> 160 us
  local copies, waits for them, and re-layouts: 5.19 us -> 14.3 us
    pallas_call x1, Pallas kernels: 144 us -> 117 us  [band_depth(): pl.pallas_call(band_kernel, out_shape=(jax.ShapeDtypeStruct((16, ROWS, 12...]
    unnamed x11 -> x14, local copies, waits for them, and re-layouts: 4.57 us -> 9.1 us
    pallas_call x1, Pallas kernels: 39.5 us -> 42.6 us  [share(): pl.pallas_call(share_kernel, out_shape=(jax.ShapeDtypeStruct((SEGS, 32, W...]
    reshape x0 -> x6, local copies, waits for them, and re-layouts: none -> 3.02 us  [the longest x3 2.43 us: by_lane(): return a.reshape(ROWS, 128, 16).transpose(2, 0, 1)]
where the time goes in v1:
time: 185 us
  Pallas kernels  160 us (86%)
  local copies, waits for them, and re-layouts  14.3 us (8%)
  blocking collectives  6.77 us (4%)
  other arithmetic  2.94 us (2%)
    pallas_call x1, Pallas kernels, band_depth(): pl.pallas_call(band_kernel, out_shape=(jax.ShapeDtypeStruct((16, ROWS, 12...  117 us
    pallas_call x1, Pallas kernels, share(): pl.pallas_call(share_kernel, out_shape=(jax.ShapeDtypeStruct((SEGS, 32, W...  42.6 us
    unnamed x14, local copies, waits for them, and re-layouts  9.1 us
    unnamed x1, blocking collectives  6.77 us

profile of v1, /device:TPU:1, one launch (start us, length us, event | category | flops | bytes accessed | tf_op | source)
XLA Modules:
  0.0 185.1 jit_solution(5731734442878287875)
XLA Ops:
  0.0 0.7 copy-done.2
  0.7 0.8 convert_reduce_fusion.1
  1.5 0.6 copy-done.3
  2.1 0.6 dynamic-slice
  3.4 0.2 dynamic-update-slice
  3.6 6.8 %all-reduce = f32[128]{0:T(128)S(1)} all-reduce(f32[128]{0:T(128)S(1)} %dynamic-update-slice), channel_id=1, replica_groups=mesh['seg'=32,'los'=4] {'los'}, use_global_device_ids=true, to_apply=%add | all-reduce | flops 128 | bytes 1024
  10.8 1.6 copy.21
  12.4 0.4 copy.22
  12.8 1.6 copy.23
  14.3 0.4 copy.24
  14.8 2.5 %copy.25 = f32[1,128,2048]{1,2,0:T(8,128)} copy(f32[1,128,2048]{2,1,0:T(8,128)} %param.7) | data formatting | bytes 2097152 | tf_op args[2]
  17.3 1.6 copy.26
  18.9 117.0 %band.1 = (f32[16,128,128]{2,1,0:T(8,128)S(1)}, f32[16,128,128]{2,1,0:T(8,128)S(1)}) custom-call(s32[128]{0:T(128)S(1)} %select_reduce_fusion.1.perm, s32[128]{0:T(128)S(1)} %convert_element_type.11.reach, f32[16,128,128]{2,1,0:T(8,128)S(1)} %bitcast.15, f32[16,128,128]{2,1,0:T(8,128)S(1)} %bitcast.16, f32[16,128,128]{2,1,0:T(8,128)S(1)} %bitcast.17), custom_call_target="tpu_custom_call" | custom-call | tf_op jit(solution)/shard_map/band/pallas_call | solution.py:140
  135.9 0.4 slice_bitcast_fusion
  136.3 0.6 copy-done
  136.9 0.3 copy.28
  137.4 0.3 copy.29
  137.8 0.7 copy-done.1
  138.6 0.5 copy.27
  139.1 0.3 copy.30.tau
  139.4 42.6 %share.1 = (f32[32,32,256]{2,1,0:T(8,128)S(1)}, f32[8,128]{1,0:T(8,128)S(1)}) custom-call(f32[128,2048]{1,0:T(8,128)S(1)} %copy.30.tau, f32[128,512]{1,0:T(8,128)S(1)} %copy.31.right, f32[128,512]{1,0:T(8,128)S(1)} %copy.32.left), custom_call_target="tpu_custom_call" | custom-call | tf_op jit(solution)/shard_map/share/pallas_call | solution.py:323
  182.1 0.6 gather_fusion
  182.7 0.6 reduce_sum.49
  184.0 1.1 select_multiply_fusion
  (14 shorter events, 0.7 us)
Async XLA Ops:
  0.0 0.7 copy-start.2
  1.5 0.7 copy-start.3
  135.9 1.0 copy-start
  137.4 1.2 copy-start.1

commit v2 on v1

--- a/solution.py
+++ b/solution.py
@@ -19,7 +19,67 @@
 F32 = jnp.float32
 
 
-def band_kernel(perm, reach, d_ref, t_ref, v_ref, tau_ref, edge_ref, W, C, NB, Q, M, Zb, S, E):
+def order_kernel(lookup, extent, order, tile, tiles, send, recv):
+    seg, los = lax.axis_index("seg"), lax.axis_index("los")
+    barrier = pltpu.get_barrier_semaphore()
+    for j in range(1, LOSS):
+        pl.semaphore_signal(barrier, inc=1, device_id=(seg, lax.rem(los + j, LOSS)), device_id_type=MESH)
+    pl.semaphore_wait(barrier, LOSS - 1)
+    row = jnp.int32(0)
+    for i in range(SEGS):
+        row = jnp.where(lookup[i] == seg, i, row)
+    tile[...] = jnp.zeros((8, 128), F32)
+    tile[0:1, 0:32] = extent[pl.ds(row, 1), :].astype(F32)
+    copies = [
+        pltpu.make_async_remote_copy(
+            src_ref=tile, dst_ref=tiles.at[j - 1], send_sem=send.at[j - 1], recv_sem=recv.at[j - 1],
+            device_id=(seg, lax.rem(los + j, LOSS)), device_id_type=MESH,
+        )
+        for j in range(1, LOSS)
+    ]
+    for copy in copies:
+        copy.start()
+    part = lax.broadcasted_iota(jnp.int32, (1, 128), 1) // 32
+    for copy in copies:
+        copy.wait_recv()
+    h = jnp.zeros((1, 128), F32)
+    for j in range(LOSS):
+        values = (tile if j == 0 else tiles.at[j - 1])[0:1, :]
+        owner = lax.rem(los + LOSS - j, LOSS)
+        for l in range(LOSS):
+            h = h + jnp.where(jnp.logical_and(part == l, owner == l), pltpu.roll(values, 32 * l, 1) if l else values, 0.0)
+    i = lax.broadcasted_iota(jnp.int32, (128, 128), 0)
+    j = lax.broadcasted_iota(jnp.int32, (128, 128), 1)
+    across = jnp.broadcast_to(h, (128, 128))
+    down = jnp.sum(jnp.where(i == j, across, 0.0), axis=1, keepdims=True)
+    below = jnp.logical_or(across < down, jnp.logical_and(across == down, j < i))
+    rank = jnp.sum(jnp.where(below, 1.0, 0.0), axis=1, keepdims=True)
+    hot = rank == j.astype(F32)
+    order[0:1, :] = jnp.sum(jnp.where(hot, i.astype(F32), 0.0), axis=0, keepdims=True).astype(jnp.int32)
+    order[1:2, :] = jnp.sum(jnp.where(hot, down, 0.0), axis=0, keepdims=True).astype(jnp.int32)
+    for copy in copies:
+        copy.wait_send()
+
+
+def sightline_order(lookup, extent):
+    vmem = pl.BlockSpec(memory_space=pltpu.VMEM)
+    return pl.pallas_call(
+        order_kernel,
+        out_shape=jax.ShapeDtypeStruct((2, ROWS), jnp.int32),
+        in_specs=[pl.BlockSpec(memory_space=pltpu.SMEM), vmem],
+        out_specs=vmem,
+        scratch_shapes=[
+            pltpu.VMEM((8, 128), F32),
+            pltpu.VMEM((3, 8, 128), F32),
+            pltpu.SemaphoreType.DMA((3,)),
+            pltpu.SemaphoreType.DMA((3,)),
+        ],
+        compiler_params=pltpu.CompilerParams(collective_id=1, has_side_effects=True, vmem_limit_bytes=4 << 20),
+        name="order",
+    )(lookup, extent)
+
+
+def band_kernel(table, d_ref, t_ref, v_ref, tau_ref, edge_ref, W, C, NB, N4, Q, M, Zb, S, E):
     lane = lax.broadcasted_iota(jnp.int32, (8, 128), 1)
     sub = lax.broadcasted_iota(jnp.int32, (8, 128), 0)
     zero = jnp.zeros((8, 128), F32)
@@ -27,7 +87,7 @@
     def gather(g, _):
         at = pl.ds(pl.multiple_of(g * 16, 16), 16)
         for i in range(8):
-            y = perm[g * 8 + i]
+            y = table[0, g * 8 + i]
             W[at, i : i + 1, :] = d_ref[:, pl.ds(y, 1), :]
             NB[at, i : i + 1, :] = t_ref[:, pl.ds(y, 1), :]
             C[at, i : i + 1, :] = v_ref[:, pl.ds(y, 1), :]
@@ -41,8 +101,9 @@
             warmth = NB[a]
             contrast = W[a]
             nb = (-LOG2E / 169.0) / warmth
-            C[a] = C[a] + float(t)
+            C[a] = 0.5 * (C[a] + float(t))
             NB[a] = nb
+            N4[a] = 4.0 * nb
             Q[a] = jnp.exp2(nb + nb)
             W[a] = ((0.3 / 13.0) * jnp.exp2(-1.2 * jnp.log2(warmth))) * (contrast * contrast)
             S[a] = zero
@@ -54,9 +115,9 @@
     def group(g, _):
         hv = zero
         for i in range(8):
-            hv = jnp.where(sub == i, reach[g * 8 + i].astype(F32), hv)
-        kout = lax.div(reach[g * 8 + 7] + 15, 16)
-        kin = lax.div(reach[g * 8] - 15, 16)
+            hv = jnp.where(sub == i, table[1, g * 8 + i].astype(F32), hv)
+        kout = lax.div(table[1, g * 8 + 7] + 15, 16)
+        kin = lax.div(table[1, g * 8] - 15, 16)
         base = g * 16
         for r in range(16):
             Zb[1, r] = zero
@@ -73,9 +134,8 @@
             for s in range(16):
                 nb = NB[base + s]
                 x = kf - C[base + s]
-                m = nb * x
-                A = W[base + s] * jnp.exp2(m * x)
-                m2 = m + m
+                m2 = N4[base + s] * x
+                A = W[base + s] * jnp.exp2(m2 * x)
                 R = jnp.exp2(m2 + nb)
                 U = jnp.exp2(nb - m2)
                 q = Q[base + s]
@@ -97,26 +157,36 @@
                     if i < 8:
                         U = U * q
 
-        def body(side, where, n, carry):
-            before, dst = carry
-            sk = where(n)
+        def step(side, sk, before, dst):
             if side:
                 hk = hv - (16 * side * sk).astype(F32)
                 for i in range(31):
                     M[i] = jnp.where(hk >= float(side * (i - 15)), 1.0, 0.0)
             Z = [None] * 16
             place(dst, before)
-            cells(Z, (16 * sk + 8).astype(F32), side)
+            cells(Z, (8 * sk + 4).astype(F32), side)
             for r in range(16):
                 Zb[dst, r] = Z[r]
+
+        def edge_step(side, where, n, carry):
+            before, dst = carry
+            sk = where(n)
+            step(side, sk, before, dst)
             return sk, 1 - dst
 
+        def two_steps(n, carry):
+            before, dst = carry
+            one = jnp.where(2 * n < kin, 2 * n - kin, 2 * kin - 2 * n)
+            two = jnp.where(2 * n + 1 < kin, 2 * n + 1 - kin, 2 * kin - 2 * n - 1)
+            step(0, one, before, dst)
+            step(0, two, one, 1 - dst)
+            return two, dst
+
         carry = (jnp.int32(0), jnp.int32(0))
-        carry = lax.fori_loop(0, kout - kin, functools.partial(body, -1, lambda n: n - kout), carry)
-        carry = lax.fori_loop(0, kout - kin, functools.partial(body, 1, lambda n: kout - n), carry)
-        carry = lax.fori_loop(
-            0, 2 * kin + 1, functools.partial(body, 0, lambda n: jnp.where(n < kin, n - kin, 2 * kin - n)), carry
-        )
+        carry = lax.fori_loop(0, kout - kin, functools.partial(edge_step, -1, lambda n: n - kout), carry)
+        carry = lax.fori_loop(0, kout - kin, functools.partial(edge_step, 1, lambda n: kout - n), carry)
+        carry = lax.fori_loop(0, kin, two_steps, carry)
+        carry = edge_step(0, lambda n: jnp.int32(0), 0, carry)
         fin = 1 - carry[1]
         for r in range(16):
             S[base + r] = S[base + r] + Zb[fin, r]
@@ -127,26 +197,26 @@
     def scatter(g, _):
         at = pl.ds(pl.multiple_of(g * 16, 16), 16)
         for i in range(8):
-            y = perm[g * 8 + i]
+            y = table[0, g * 8 + i]
             tau_ref[:, pl.ds(y, 1), :] = S[at, i : i + 1, :]
             edge_ref[:, pl.ds(y, 1), :] = E[at, i : i + 1, :]
         return 0
 
     lax.fori_loop(0, GROUPS, scatter, 0)
 
-def band_depth(perm, reach, d, t, v):
+def band_depth(order, d, t, v):
     whole = pl.BlockSpec((16, ROWS, 128), lambda i, *_: (0, 0, 0))
     table = pltpu.VMEM((GROUPS * 16, 8, 128), F32)
     return pl.pallas_call(
         band_kernel,
         out_shape=(jax.ShapeDtypeStruct((16, ROWS, 128), F32),) * 2,
         grid_spec=pltpu.PrefetchScalarGridSpec(
-            num_scalar_prefetch=2, grid=(1,), in_specs=[whole] * 3, out_specs=[whole] * 2,
-            scratch_shapes=[table] * 4 + [pltpu.VMEM((31, 8, 128), F32), pltpu.VMEM((2, 16, 8, 128), F32), table, table],
+            num_scalar_prefetch=1, grid=(1,), in_specs=[whole] * 3, out_specs=[whole] * 2,
+            scratch_shapes=[table] * 5 + [pltpu.VMEM((31, 8, 128), F32), pltpu.VMEM((2, 16, 8, 128), F32), table, table],
         ),
-        compiler_params=pltpu.CompilerParams(vmem_limit_bytes=40 << 20),
+        compiler_params=pltpu.CompilerParams(vmem_limit_bytes=24 << 20),
         name="band",
-    )(perm, reach, d, t, v)
+    )(order, d, t, v)
 
 
 def share_kernel(tau, right, left, got, sums_out, from_left, from_right, flux, relay, part, parts, local_sum, sums,
@@ -345,22 +415,13 @@
             dma((15,)),
             dma((15,)),
         ],
-        compiler_params=pltpu.CompilerParams(collective_id=0, has_side_effects=True, vmem_limit_bytes=24 << 20),
+        compiler_params=pltpu.CompilerParams(collective_id=0, has_side_effects=True, vmem_limit_bytes=10 << 20),
         name="share",
     )(tau, right, left)
 
 
 def per_device(contrast, warmth, velocity, semi_extent, lookup):
-    seg = lax.axis_index("seg")
-    mine = lookup == seg
-    own = jnp.sum(jnp.where(mine[:, None], semi_extent, 0).astype(F32), axis=0)
-    h = lax.all_gather(own, "los", tiled=True)
-    at = jnp.arange(ROWS)
-    below = (h[None, :] < h[:, None]) | ((h[None, :] == h[:, None]) & (at[None, :] < at[:, None]))
-    rank = jnp.sum(below.astype(jnp.int32), axis=1)
-    hot = rank[:, None] == at[None, :]
-    perm = jnp.sum(jnp.where(hot, at[:, None], 0), axis=0).astype(jnp.int32)
-    reach = jnp.sum(jnp.where(hot, h[:, None], 0.0), axis=0).astype(jnp.int32)
+    order = sightline_order(lookup, semi_extent)
 
     def by_lane(a):
         return a.reshape(ROWS, 128, 16).transpose(2, 0, 1)
@@ -368,7 +429,7 @@
     def in_order(a):
         return a.transpose(1, 2, 0).reshape(ROWS, -1)
 
-    tau, edge = band_depth(perm, reach, by_lane(contrast), by_lane(warmth), by_lane(velocity))
+    tau, edge = band_depth(order, by_lane(contrast), by_lane(warmth), by_lane(velocity))
     got, sums = share(in_order(tau), in_order(edge[:, :, :32]), in_order(edge[:, :, 96:]))
     scale = CELLS / jnp.sum(sums)
     return jnp.take(got, lookup, axis=0) * scale

time: 185 us -> 175 us (0.946)
  blocking collectives: 6.77 us -> 0 us
    unnamed x1 -> x0, blocking collectives: 6.77 us -> none
    pallas_call x0 -> x1, Pallas kernels: none -> 5.54 us  [sightline_order(): pl.pallas_call(order_kernel, out_shape=jax.ShapeDtypeStruct((2, ROWS), jn...]
    pallas_call x1, Pallas kernels: 42.6 us -> 38.5 us  [share(): pl.pallas_call(share_kernel, out_shape=(jax.ShapeDtypeStruct((SEGS, 32, W...]
    pallas_call x1, Pallas kernels: 117 us -> 115 us  [band_depth(): pl.pallas_call(band_kernel, out_shape=(jax.ShapeDtypeStruct((16, ROWS, 12...]
    unnamed x14 -> x11, local copies, waits for them, and re-layouts: 9.1 us -> 7.62 us
where the time goes in v2:
time: 175 us; the launch traced here: 174 us
  Pallas kernels  159 us (91%)
  local copies, waits for them, and re-layouts  12.8 us (7%)
    pallas_call x1, Pallas kernels, band_depth(): pl.pallas_call(band_kernel, out_shape=(jax.ShapeDtypeStruct((16, ROWS, 12...  115 us
    pallas_call x1, Pallas kernels, share(): pl.pallas_call(share_kernel, out_shape=(jax.ShapeDtypeStruct((SEGS, 32, W...  38.5 us
    unnamed x11, local copies, waits for them, and re-layouts  7.62 us
    pallas_call x1, Pallas kernels, sightline_order(): pl.pallas_call(order_kernel, out_shape=jax.ShapeDtypeStruct((2, ROWS), jn...  5.54 us

profile of v2, /device:TPU:1, one launch (start us, length us, event | category | flops | bytes accessed | tf_op | source)
XLA Modules:
  0.0 174.0 jit_solution(17998570882292781311)
XLA Ops:
  0.0 1.5 copy.9
  1.6 0.4 copy.10
  2.0 1.6 copy.11
  3.5 0.4 copy.12
  4.0 2.5 %copy.13 = f32[1,128,2048]{1,2,0:T(8,128)} copy(f32[1,128,2048]{2,1,0:T(8,128)} %param.7) | data formatting | bytes 2097152 | tf_op args[2]
  6.5 1.6 copy.14
  8.1 0.0 copy-start.3
  8.1 0.6 copy-done.3
  8.8 5.5 %order.1.table = s32[2,128]{1,0:T(2,128)S(1)} custom-call(s32[32]{0:T(128)S(1)} %copy-done.3, s32[32,32]{1,0:T(8,128)S(1)} %copy-done.2), custom_call_target="tpu_custom_call" | custom-call | tf_op jit(solution)/shard_map/order/pallas_call | solution.py:66
  14.3 114.6 %band.1 = (f32[16,128,128]{2,1,0:T(8,128)S(1)}, f32[16,128,128]{2,1,0:T(8,128)S(1)}) custom-call(s32[2,128]{1,0:T(2,128)S(1)} %order.1.table, f32[16,128,128]{2,1,0:T(8,128)S(1)} %bitcast.14, f32[16,128,128]{2,1,0:T(8,128)S(1)} %bitcast.15, f32[16,128,128]{2,1,0:T(8,128)S(1)} %bitcast.16), custom_call_target="tpu_custom_call" | custom-call | tf_op jit(solution)/shard_map/band/pallas_call | solution.py:210
  128.9 0.4 slice_bitcast_fusion
  129.3 0.6 copy-done
  129.9 0.3 copy.16
  130.2 0.1 copy.19.right
  130.3 0.0 copy-start.1
  130.4 0.3 copy.17
  130.7 0.1 copy.20.left
  130.8 0.7 copy-done.1
  131.6 0.5 copy.15
  132.1 0.3 copy.18.tau
  132.4 38.5 %share.1 = (f32[32,32,256]{2,1,0:T(8,128)S(1)}, f32[8,128]{1,0:T(8,128)S(1)}) custom-call(f32[128,2048]{1,0:T(8,128)S(1)} %copy.18.tau, f32[128,512]{1,0:T(8,128)S(1)} %copy.19.right, f32[128,512]{1,0:T(8,128)S(1)} %copy.20.left), custom_call_target="tpu_custom_call" | custom-call | tf_op jit(solution)/shard_map/share/pallas_call | solution.py:393
  170.9 0.6 gather_fusion
  171.6 0.6 reduce_sum.9
  172.9 1.1 select_multiply_fusion
  (6 shorter events, 0.0 us)
Async XLA Ops:
  6.5 1.6 copy-start.2
  8.1 0.7 copy-start.3
  128.9 1.0 copy-start
  130.3 1.2 copy-start.1

commit v3 on v2

--- a/solution.py
+++ b/solution.py
@@ -19,7 +19,10 @@
 F32 = jnp.float32
 
 
-def order_kernel(lookup, extent, order, tile, tiles, send, recv):
+def order_kernel(lookup, extent, d, t, v, order, d_out, t_out, v_out, fields, cells, tile, tiles, load, send, recv):
+    loads = [pltpu.make_async_copy(ref, fields.at[n], load.at[n]) for n, ref in enumerate((d, t, v))]
+    for copy in loads:
+        copy.start()
     seg, los = lax.axis_index("seg"), lax.axis_index("los")
     barrier = pltpu.get_barrier_semaphore()
     for j in range(1, LOSS):
@@ -39,6 +42,17 @@
     ]
     for copy in copies:
         copy.start()
+    for n, out in enumerate((d_out, t_out, v_out)):
+        loads[n].wait()
+
+        def columns(m, _):
+            block = fields[n, :, pl.ds(pl.multiple_of(m * 128, 128), 128)].T
+            cells[pl.ds(pl.multiple_of(m * 8, 8), 8)] = block.reshape(8, 16, 128)
+            return 0
+
+        lax.fori_loop(0, 16, columns, 0)
+        for i in range(16):
+            out[i] = cells[:, i, :].T
     part = lax.broadcasted_iota(jnp.int32, (1, 128), 1) // 32
     for copy in copies:
         copy.wait_recv()
@@ -61,22 +75,27 @@
         copy.wait_send()
 
 
-def sightline_order(lookup, extent):
+def sightline_order(lookup, extent, d, t, v):
     vmem = pl.BlockSpec(memory_space=pltpu.VMEM)
+    there = pl.BlockSpec(memory_space=pl.ANY)
+    by_lane = jax.ShapeDtypeStruct((16, ROWS, 128), F32)
     return pl.pallas_call(
         order_kernel,
-        out_shape=jax.ShapeDtypeStruct((2, ROWS), jnp.int32),
-        in_specs=[pl.BlockSpec(memory_space=pltpu.SMEM), vmem],
-        out_specs=vmem,
+        out_shape=(jax.ShapeDtypeStruct((2, ROWS), jnp.int32), by_lane, by_lane, by_lane),
+        in_specs=[pl.BlockSpec(memory_space=pltpu.SMEM), vmem, there, there, there],
+        out_specs=(vmem,) * 4,
         scratch_shapes=[
+            pltpu.VMEM((3, ROWS, LENGTH), F32),
+            pltpu.VMEM((128, 16, 128), F32),
             pltpu.VMEM((8, 128), F32),
             pltpu.VMEM((3, 8, 128), F32),
             pltpu.SemaphoreType.DMA((3,)),
             pltpu.SemaphoreType.DMA((3,)),
+            pltpu.SemaphoreType.DMA((3,)),
         ],
-        compiler_params=pltpu.CompilerParams(collective_id=1, has_side_effects=True, vmem_limit_bytes=4 << 20),
+        compiler_params=pltpu.CompilerParams(collective_id=1, has_side_effects=True, vmem_limit_bytes=50 << 20),
         name="order",
-    )(lookup, extent)
+    )(lookup, extent, d, t, v)
 
 
 def band_kernel(table, d_ref, t_ref, v_ref, tau_ref, edge_ref, W, C, NB, N4, Q, M, Zb, S, E):
@@ -186,7 +205,7 @@
         carry = lax.fori_loop(0, kout - kin, functools.partial(edge_step, -1, lambda n: n - kout), carry)
         carry = lax.fori_loop(0, kout - kin, functools.partial(edge_step, 1, lambda n: kout - n), carry)
         carry = lax.fori_loop(0, kin, two_steps, carry)
-        carry = edge_step(0, lambda n: jnp.int32(0), 0, carry)
+        carry = lax.fori_loop(kin, kin + 1, functools.partial(edge_step, 0, lambda n: jnp.int32(0)), carry)
         fin = 1 - carry[1]
         for r in range(16):
             S[base + r] = S[base + r] + Zb[fin, r]
@@ -421,15 +440,15 @@
 
 
 def per_device(contrast, warmth, velocity, semi_extent, lookup):
-    order = sightline_order(lookup, semi_extent)
-
-    def by_lane(a):
-        return a.reshape(ROWS, 128, 16).transpose(2, 0, 1)
+    shape = (ROWS, LENGTH)
+    order, d, t, v = sightline_order(
+        lookup, semi_extent, contrast.reshape(shape), warmth.reshape(shape), velocity.reshape(shape)
+    )
 
     def in_order(a):
         return a.transpose(1, 2, 0).reshape(ROWS, -1)
 
-    tau, edge = band_depth(order, by_lane(contrast), by_lane(warmth), by_lane(velocity))
+    tau, edge = band_depth(order, d, t, v)
     got, sums = share(in_order(tau), in_order(edge[:, :, :32]), in_order(edge[:, :, 96:]))
     scale = CELLS / jnp.sum(sums)
     return jnp.take(got, lookup, axis=0) * scale

time: 175 us -> 173 us (0.989)
  local copies, waits for them, and re-layouts: 12.8 us -> 6.28 us
  Pallas kernels: 159 us -> 164 us
    unnamed x11 -> x4, local copies, waits for them, and re-layouts: 7.62 us -> 1.37 us
    pallas_call x1, Pallas kernels: 5.54 us -> 10.6 us  [sightline_order(): pl.pallas_call(order_kernel, out_shape=(jax.ShapeDtypeStruct((2, ROWS), j...]
    pallas_call x1, Pallas kernels: 115 us -> 112 us  [band_depth(): pl.pallas_call(band_kernel, out_shape=(jax.ShapeDtypeStruct((16, ROWS, 12...]
    pallas_call x1, Pallas kernels: 38.5 us -> 41 us  [share(): pl.pallas_call(share_kernel, out_shape=(jax.ShapeDtypeStruct((SEGS, 32, W...]
    reshape x3 -> x0, local copies, waits for them, and re-layouts: 2.44 us -> none  [by_lane(): return a.reshape(ROWS, 128, 16).transpose(2, 0, 1)]
    transpose x4, local copies, waits for them, and re-layouts: 1.53 us -> 3.71 us  [in_order(): return a.transpose(1, 2, 0).reshape(ROWS, -1)]
where the time goes in v3:
time: 173 us; the launch traced here: 172 us
  Pallas kernels  164 us (95%)
  local copies, waits for them, and re-layouts  6.28 us (4%)
  other arithmetic  1.74 us (1%)
    pallas_call x1, Pallas kernels, band_depth(): pl.pallas_call(band_kernel, out_shape=(jax.ShapeDtypeStruct((16, ROWS, 12...  112 us
    pallas_call x1, Pallas kernels, share(): pl.pallas_call(share_kernel, out_shape=(jax.ShapeDtypeStruct((SEGS, 32, W...  41 us
    pallas_call x1, Pallas kernels, sightline_order(): pl.pallas_call(order_kernel, out_shape=(jax.ShapeDtypeStruct((2, ROWS), j...  10.6 us
    transpose x4, local copies, waits for them, and re-layouts, in_order(): return a.transpose(1, 2, 0).reshape(ROWS, -1)  3.71 us

profile of v3, /device:TPU:1, one launch (start us, length us, event | category | flops | bytes accessed | tf_op | source)
XLA Modules:
  0.0 172.4 jit_solution(11496034433733911866)
XLA Ops:
  0.0 0.0 copy-start.1
  0.0 0.7 copy-done.1
  0.7 0.0 copy-start
  0.7 0.7 copy-done
  1.4 10.6 %order.1 = (s32[2,128]{1,0:T(2,128)S(1)}, f32[16,128,128]{2,1,0:T(8,128)S(1)}, f32[16,128,128]{2,1,0:T(8,128)S(1)}, f32[16,128,128]{2,1,0:T(8,128)S(1)}) custom-call(s32[32]{0:T(128)S(1)} %copy-done.1, s32[32,32]{1,0:T(8,128)S(1)} %copy-done, f32[128,2048]{1,0:T(8,128)} %bitcast.15, f32[128,2048]{1,0:T(8,128)} %bitcast.16, f32[128,2048]{1,0:T(8,128)} %bitcast.17), custom_call_target="tpu_custom_call" | custom-call | tf_op jit(solution)/shard_map/order/pallas_call | solution.py:82
  12.0 111.9 %band.1 = (f32[16,128,128]{2,1,0:T(8,128)S(1)}, f32[16,128,128]{2,1,0:T(8,128)S(1)}) custom-call(s32[2,128]{1,0:T(2,128)S(1)} %get-tuple-element.13.table, f32[16,128,128]{2,1,0:T(8,128)S(1)} %get-tuple-element.14.d_ref, f32[16,128,128]{2,1,0:T(8,128)S(1)} %get-tuple-element.15.t_ref, f32[16,128,128]{2,1,0:T(8,128)S(1)} %get-tuple-element.16.v_ref), custom_call_target="tpu_custom_call" | custom-call | tf_op jit(solution)/shard_map/band/pallas_call | solution.py:229
  123.9 1.3 slice_bitcast_fusion
  125.2 1.6 copy.10
  126.8 0.1 copy.13.right
  126.9 0.3 copy.11
  127.3 0.1 copy.14.left
  127.4 0.5 copy.9
  127.9 0.3 copy.12.tau
  128.3 41.0 %share.1 = (f32[32,32,256]{2,1,0:T(8,128)S(1)}, f32[8,128]{1,0:T(8,128)S(1)}) custom-call(f32[128,2048]{1,0:T(8,128)S(1)} %copy.12.tau, f32[128,512]{1,0:T(8,128)S(1)} %copy.13.right, f32[128,512]{1,0:T(8,128)S(1)} %copy.14.left), custom_call_target="tpu_custom_call" | custom-call | tf_op jit(solution)/shard_map/share/pallas_call | solution.py:412
  169.3 0.6 gather_fusion
  170.0 0.6 reduce_sum.9
  171.3 1.1 select_multiply_fusion
  (3 shorter events, 0.0 us)
Async XLA Ops:
  0.0 0.7 copy-start.1
  0.7 0.7 copy-start

commit v4 on v3

--- a/solution.py
+++ b/solution.py
@@ -27,6 +27,20 @@
     barrier = pltpu.get_barrier_semaphore()
     for j in range(1, LOSS):
         pl.semaphore_signal(barrier, inc=1, device_id=(seg, lax.rem(los + j, LOSS)), device_id_type=MESH)
+
+    def turn(n):
+        loads[n].wait()
+
+        def columns(m, _):
+            block = fields[n, :, pl.ds(pl.multiple_of(m * 128, 128), 128)].T
+            cells[pl.ds(pl.multiple_of(m * 8, 8), 8)] = block.reshape(8, 16, 128)
+            return 0
+
+        lax.fori_loop(0, 16, columns, 0)
+        for i in range(16):
+            (d_out, t_out, v_out)[n][i] = cells[:, i, :].T
+
+    turn(0)
     pl.semaphore_wait(barrier, LOSS - 1)
     row = jnp.int32(0)
     for i in range(SEGS):
@@ -42,17 +56,8 @@
     ]
     for copy in copies:
         copy.start()
-    for n, out in enumerate((d_out, t_out, v_out)):
-        loads[n].wait()
-
-        def columns(m, _):
-            block = fields[n, :, pl.ds(pl.multiple_of(m * 128, 128), 128)].T
-            cells[pl.ds(pl.multiple_of(m * 8, 8), 8)] = block.reshape(8, 16, 128)
-            return 0
-
-        lax.fori_loop(0, 16, columns, 0)
-        for i in range(16):
-            out[i] = cells[:, i, :].T
+    turn(1)
+    turn(2)
     part = lax.broadcasted_iota(jnp.int32, (1, 128), 1) // 32
     for copy in copies:
         copy.wait_recv()
@@ -238,7 +243,7 @@
     )(order, d, t, v)
 
 
-def share_kernel(tau, right, left, got, sums_out, from_left, from_right, flux, relay, part, parts, local_sum, sums,
+def share_kernel(tau, edge, got, sums_out, right, left, from_left, from_right, cells, flux, relay, part, parts, local_sum, sums,
                  edge_send, edge_recv, a_send, a_recv, b_send, b_recv, p_send, p_recv, q_send, q_recv):
     seg, los = lax.axis_index("seg"), lax.axis_index("los")
     y, zh, x = lax.div(seg, 8), lax.rem(lax.div(seg, 4), 2), lax.rem(seg, 4)
@@ -264,6 +269,10 @@
         signal(y * 8 + h * 4 + x, l)
     for i in range(1, 16):
         signal(plane(i // 4, i % 4), los)
+    for i in range(16):
+        block = edge[i].T
+        right[:, i, :] = block[0:32]
+        left[:, i, :] = block[96:128]
     pl.semaphore_wait(barrier, 22)
 
     def remote(src, dst, send, recv, s, l):
@@ -277,24 +286,26 @@
     ]
     for copy in edges:
         copy.start()
+    for i in range(16):
+        cells[:, i, :] = tau[i].T
+
+    def depth_of(m):
+        return cells[m * 8 : m * 8 + 8].reshape(128, 128)
+
+    def take_flux(m, depth):
+        value = jnp.exp(-depth)
+        flux[:, m * 128 : (m + 1) * 128] = value.T
+        return jnp.sum(value.reshape(16, 8, 128), axis=0)
+
+    total = jnp.zeros((8, 128), F32)
+    for m in range(4, 12):
+        total = total + take_flux(m, depth_of(m))
     for copy in edges:
         copy.wait_recv()
-
-    def rows_of(i, total):
-        rows = pl.ds(pl.multiple_of(i * 8, 8), 8)
-        for m in range(16):
-            cols = pl.ds(m * 128, 128)
-            depth = tau[rows, cols]
-            if m < 4:
-                depth = depth + from_left[rows, cols]
-            if m >= 12:
-                depth = depth + from_right[rows, pl.ds((m - 12) * 128, 128)]
-            value = jnp.exp(-depth)
-            flux[rows, cols] = value
-            total = total + value
-        return total
-
-    part[...] = lax.fori_loop(0, GROUPS, rows_of, jnp.zeros((8, 128), F32))
+    for m in range(4):
+        total = total + take_flux(m, depth_of(m) + from_left[m * 8 : m * 8 + 8].reshape(128, 128))
+        total = total + take_flux(m + 12, depth_of(m + 12) + from_right[m * 8 : m * 8 + 8].reshape(128, 128))
+    part[...] = total
 
     def a_part(d):
         h, l = column(d)
@@ -406,17 +417,21 @@
             b_copy(d, 0).wait_send()
 
 
-def share(tau, right, left):
+def share(tau, edge):
     vmem = pl.BlockSpec(memory_space=pltpu.VMEM)
     dma = pltpu.SemaphoreType.DMA
+    side = pltpu.VMEM((REACH // 16, 16, ROWS), F32)
     return pl.pallas_call(
         share_kernel,
         out_shape=(jax.ShapeDtypeStruct((SEGS, 32, WIDE), F32), jax.ShapeDtypeStruct((8, 128), F32)),
-        in_specs=[vmem] * 3,
+        in_specs=[vmem] * 2,
         out_specs=(pl.BlockSpec(memory_space=pl.ANY), vmem),
         scratch_shapes=[
-            pltpu.VMEM((ROWS, REACH), F32),
-            pltpu.VMEM((ROWS, REACH), F32),
+            side,
+            side,
+            side,
+            side,
+            pltpu.VMEM((128, 16, ROWS), F32),
             pltpu.VMEM((ROWS, LENGTH), F32),
             pltpu.VMEM((8, 32, 1024), F32),
             pltpu.VMEM((8, 128), F32),
@@ -434,9 +449,31 @@
             dma((15,)),
             dma((15,)),
         ],
-        compiler_params=pltpu.CompilerParams(collective_id=0, has_side_effects=True, vmem_limit_bytes=10 << 20),
+        compiler_params=pltpu.CompilerParams(collective_id=0, has_side_effects=True, vmem_limit_bytes=12 << 20),
         name="share",
-    )(tau, right, left)
+    )(tau, edge)
+
+
+def finish_kernel(lookup, got, sums, flux):
+    scale = CELLS / jnp.sum(sums[...], axis=(0, 1), keepdims=True)
+
+    def row(k, _):
+        flux[k] = got[lookup[k]] * scale
+        return 0
+
+    lax.fori_loop(0, SEGS, row, 0)
+
+
+def finish(lookup, got, sums):
+    vmem = pl.BlockSpec(memory_space=pltpu.VMEM)
+    return pl.pallas_call(
+        finish_kernel,
+        out_shape=jax.ShapeDtypeStruct((SEGS, 32, WIDE), F32),
+        in_specs=[pl.BlockSpec(memory_space=pltpu.SMEM), vmem, vmem],
+        out_specs=vmem,
+        compiler_params=pltpu.CompilerParams(vmem_limit_bytes=8 << 20),
+        name="finish",
+    )(lookup, got, sums)
 
 
 def per_device(contrast, warmth, velocity, semi_extent, lookup):
@@ -445,13 +482,9 @@
         lookup, semi_extent, contrast.reshape(shape), warmth.reshape(shape), velocity.reshape(shape)
     )
 
-    def in_order(a):
-        return a.transpose(1, 2, 0).reshape(ROWS, -1)
-
     tau, edge = band_depth(order, d, t, v)
-    got, sums = share(in_order(tau), in_order(edge[:, :, :32]), in_order(edge[:, :, 96:]))
-    scale = CELLS / jnp.sum(sums)
-    return jnp.take(got, lookup, axis=0) * scale
+    got, sums = share(tau, edge)
+    return finish(lookup, got, sums)
 
 
 def solution(mesh):

time: 173 us -> 167 us (0.965)
  local copies, waits for them, and re-layouts: 6.28 us -> 1.37 us
  Pallas kernels: 164 us -> 166 us
  other arithmetic: 1.74 us -> 0 us
    transpose x4 -> x0, local copies, waits for them, and re-layouts: 3.71 us -> none  [in_order(): return a.transpose(1, 2, 0).reshape(ROWS, -1)]
    pallas_call x1, Pallas kernels: 112 us -> 115 us  [band_depth(): pl.pallas_call(band_kernel, out_shape=(jax.ShapeDtypeStruct((16, ROWS, 12...]
    pallas_call x0 -> x1, Pallas kernels: none -> 1.88 us  [finish(): pl.pallas_call(finish_kernel, out_shape=jax.ShapeDtypeStruct((SEGS, 32, W...]
where the time goes in v4:
time: 167 us
  Pallas kernels  166 us (99%)
    pallas_call x1, Pallas kernels, band_depth(): pl.pallas_call(band_kernel, out_shape=(jax.ShapeDtypeStruct((16, ROWS, 12...  115 us
    pallas_call x1, Pallas kernels, share(): pl.pallas_call(share_kernel, out_shape=(jax.ShapeDtypeStruct((SEGS, 32, W...  39.8 us
    pallas_call x1, Pallas kernels, sightline_order(): pl.pallas_call(order_kernel, out_shape=(jax.ShapeDtypeStruct((2, ROWS), j...  8.96 us

profile of v4, /device:TPU:1, one launch (start us, length us, event | category | flops | bytes accessed | tf_op | source)
XLA Modules:
  0.0 167.0 jit_solution(2645792774513666305)
XLA Ops:
  0.0 0.0 copy-start.1
  0.0 0.7 copy-done.1
  0.7 0.0 copy-start
  0.7 0.7 copy-done
  1.4 9.0 %order.1 = (s32[2,128]{1,0:T(2,128)S(1)}, f32[16,128,128]{2,1,0:T(8,128)S(1)}, f32[16,128,128]{2,1,0:T(8,128)S(1)}, f32[16,128,128]{2,1,0:T(8,128)S(1)}) custom-call(s32[32]{0:T(128)S(1)} %copy-done.1, s32[32,32]{1,0:T(8,128)S(1)} %copy-done, f32[128,2048]{1,0:T(8,128)} %bitcast.3, f32[128,2048]{1,0:T(8,128)} %bitcast.4, f32[128,2048]{1,0:T(8,128)} %bitcast.5), custom_call_target="tpu_custom_call" | custom-call | tf_op jit(solution)/shard_map/order/pallas_call | solution.py:87
  10.3 115.0 %band.1 = (f32[16,128,128]{2,1,0:T(8,128)S(1)}, f32[16,128,128]{2,1,0:T(8,128)S(1)}) custom-call(s32[2,128]{1,0:T(2,128)S(1)} %get-tuple-element.13.table, f32[16,128,128]{2,1,0:T(8,128)S(1)} %get-tuple-element.14.d_ref, f32[16,128,128]{2,1,0:T(8,128)S(1)} %get-tuple-element.15.t_ref, f32[16,128,128]{2,1,0:T(8,128)S(1)} %get-tuple-element.16.v_ref), custom_call_target="tpu_custom_call" | custom-call | tf_op jit(solution)/shard_map/band/pallas_call | solution.py:234
  125.3 39.8 %share.1 = (f32[32,32,256]{2,1,0:T(8,128)S(1)}, f32[8,128]{1,0:T(8,128)S(1)}) custom-call(f32[16,128,128]{2,1,0:T(8,128)S(1)} %get-tuple-element.17.tau, f32[16,128,128]{2,1,0:T(8,128)S(1)} %get-tuple-element.18.edge), custom_call_target="tpu_custom_call" | custom-call | tf_op jit(solution)/shard_map/share/pallas_call | solution.py:424
  165.1 1.9 %finish.1 = f32[32,32,256]{2,1,0:T(8,128)} custom-call(s32[32]{0:T(128)S(1)} %copy-done.1, f32[32,32,256]{2,1,0:T(8,128)S(1)} %get-tuple-element.19.got, f32[8,128]{1,0:T(8,128)S(1)} %get-tuple-element.20.sums), custom_call_target="tpu_custom_call" | custom-call | tf_op jit(solution)/shard_map/finish/pallas_call | solution.py:469
Async XLA Ops:
  0.0 0.7 copy-start.1
  0.7 0.7 copy-start

commit v5 on v4

--- a/solution.py
+++ b/solution.py
@@ -31,14 +31,10 @@
     def turn(n):
         loads[n].wait()
 
-        def columns(m, _):
-            block = fields[n, :, pl.ds(pl.multiple_of(m * 128, 128), 128)].T
-            cells[pl.ds(pl.multiple_of(m * 8, 8), 8)] = block.reshape(8, 16, 128)
-            return 0
-
-        lax.fori_loop(0, 16, columns, 0)
+        for m in range(16):
+            cells[m * 128 : (m + 1) * 128] = fields[n, :, m * 128 : (m + 1) * 128].T
         for i in range(16):
-            (d_out, t_out, v_out)[n][i] = cells[:, i, :].T
+            (d_out, t_out, v_out)[n][i] = cells[pl.ds(i, 128, stride=16), :].T
 
     turn(0)
     pl.semaphore_wait(barrier, LOSS - 1)
@@ -91,7 +87,7 @@
         out_specs=(vmem,) * 4,
         scratch_shapes=[
             pltpu.VMEM((3, ROWS, LENGTH), F32),
-            pltpu.VMEM((128, 16, 128), F32),
+            pltpu.VMEM((LENGTH, ROWS), F32),
             pltpu.VMEM((8, 128), F32),
             pltpu.VMEM((3, 8, 128), F32),
             pltpu.SemaphoreType.DMA((3,)),
@@ -271,8 +267,8 @@
         signal(plane(i // 4, i % 4), los)
     for i in range(16):
         block = edge[i].T
-        right[:, i, :] = block[0:32]
-        left[:, i, :] = block[96:128]
+        right[pl.ds(i, 32, stride=16), :] = block[0:32]
+        left[pl.ds(i, 32, stride=16), :] = block[96:128]
     pl.semaphore_wait(barrier, 22)
 
     def remote(src, dst, send, recv, s, l):
@@ -287,10 +283,10 @@
     for copy in edges:
         copy.start()
     for i in range(16):
-        cells[:, i, :] = tau[i].T
+        cells[pl.ds(i, 128, stride=16), :] = tau[i].T
 
     def depth_of(m):
-        return cells[m * 8 : m * 8 + 8].reshape(128, 128)
+        return cells[m * 128 : (m + 1) * 128]
 
     def take_flux(m, depth):
         value = jnp.exp(-depth)
@@ -303,8 +299,8 @@
     for copy in edges:
         copy.wait_recv()
     for m in range(4):
-        total = total + take_flux(m, depth_of(m) + from_left[m * 8 : m * 8 + 8].reshape(128, 128))
-        total = total + take_flux(m + 12, depth_of(m + 12) + from_right[m * 8 : m * 8 + 8].reshape(128, 128))
+        total = total + take_flux(m, depth_of(m) + from_left[m * 128 : (m + 1) * 128])
+        total = total + take_flux(m + 12, depth_of(m + 12) + from_right[m * 128 : (m + 1) * 128])
     part[...] = total
 
     def a_part(d):
@@ -420,7 +416,7 @@
 def share(tau, edge):
     vmem = pl.BlockSpec(memory_space=pltpu.VMEM)
     dma = pltpu.SemaphoreType.DMA
-    side = pltpu.VMEM((REACH // 16, 16, ROWS), F32)
+    side = pltpu.VMEM((REACH, ROWS), F32)
     return pl.pallas_call(
         share_kernel,
         out_shape=(jax.ShapeDtypeStruct((SEGS, 32, WIDE), F32), jax.ShapeDtypeStruct((8, 128), F32)),
@@ -431,7 +427,7 @@
             side,
             side,
             side,
-            pltpu.VMEM((128, 16, ROWS), F32),
+            pltpu.VMEM((LENGTH, ROWS), F32),
             pltpu.VMEM((ROWS, LENGTH), F32),
             pltpu.VMEM((8, 32, 1024), F32),
             pltpu.VMEM((8, 128), F32),

time: 167 us -> 164 us (0.982)
  Pallas kernels: 166 us -> 163 us
where the time goes in v5:
time: 164 us
  Pallas kernels  163 us (99%)
    pallas_call x1, Pallas kernels, band_depth(): pl.pallas_call(band_kernel, out_shape=(jax.ShapeDtypeStruct((16, ROWS, 12...  115 us
    pallas_call x1, Pallas kernels, share(): pl.pallas_call(share_kernel, out_shape=(jax.ShapeDtypeStruct((SEGS, 32, W...  38.4 us
    pallas_call x1, Pallas kernels, sightline_order(): pl.pallas_call(order_kernel, out_shape=(jax.ShapeDtypeStruct((2, ROWS), j...  7.41 us

profile of v5, /device:TPU:1, one launch (start us, length us, event | category | flops | bytes accessed | tf_op | source)
XLA Modules:
  0.0 164.1 jit_solution(5463911463658333210)
XLA Ops:
  0.0 0.0 copy-start.1
  0.0 0.7 copy-done.1
  0.7 0.0 copy-start
  0.7 0.7 copy-done
  1.4 7.4 %order.1 = (s32[2,128]{1,0:T(2,128)S(1)}, f32[16,128,128]{2,1,0:T(8,128)S(1)}, f32[16,128,128]{2,1,0:T(8,128)S(1)}, f32[16,128,128]{2,1,0:T(8,128)S(1)}) custom-call(s32[32]{0:T(128)S(1)} %copy-done.1, s32[32,32]{1,0:T(8,128)S(1)} %copy-done, f32[128,2048]{1,0:T(8,128)} %bitcast.3, f32[128,2048]{1,0:T(8,128)} %bitcast.4, f32[128,2048]{1,0:T(8,128)} %bitcast.5), custom_call_target="tpu_custom_call" | custom-call | tf_op jit(solution)/shard_map/order/pallas_call | solution.py:83
  8.8 114.9 %band.1 = (f32[16,128,128]{2,1,0:T(8,128)S(1)}, f32[16,128,128]{2,1,0:T(8,128)S(1)}) custom-call(s32[2,128]{1,0:T(2,128)S(1)} %get-tuple-element.13.table, f32[16,128,128]{2,1,0:T(8,128)S(1)} %get-tuple-element.14.d_ref, f32[16,128,128]{2,1,0:T(8,128)S(1)} %get-tuple-element.15.t_ref, f32[16,128,128]{2,1,0:T(8,128)S(1)} %get-tuple-element.16.v_ref), custom_call_target="tpu_custom_call" | custom-call | tf_op jit(solution)/shard_map/band/pallas_call | solution.py:230
  123.7 38.4 %share.1 = (f32[32,32,256]{2,1,0:T(8,128)S(1)}, f32[8,128]{1,0:T(8,128)S(1)}) custom-call(f32[16,128,128]{2,1,0:T(8,128)S(1)} %get-tuple-element.17.tau, f32[16,128,128]{2,1,0:T(8,128)S(1)} %get-tuple-element.18.edge), custom_call_target="tpu_custom_call" | custom-call | tf_op jit(solution)/shard_map/share/pallas_call | solution.py:420
  162.2 1.9 %finish.1 = f32[32,32,256]{2,1,0:T(8,128)} custom-call(s32[32]{0:T(128)S(1)} %copy-done.1, f32[32,32,256]{2,1,0:T(8,128)S(1)} %get-tuple-element.19.got, f32[8,128]{1,0:T(8,128)S(1)} %get-tuple-element.20.sums), custom_call_target="tpu_custom_call" | custom-call | tf_op jit(solution)/shard_map/finish/pallas_call | solution.py:465
Async XLA Ops:
  0.0 0.7 copy-start.1
  0.7 0.7 copy-start

commit v6 on v5

--- a/solution.py
+++ b/solution.py
@@ -322,7 +322,7 @@
     for d in range(1, 8):
         p_copy(d).start()
     keep = pltpu.make_async_copy(a_part(0), relay.at[me], a_recv.at[me])
-    for d in (4, 2, 6, 5, 3, 7, 1):
+    for d in (2, 4, 6, 3, 5, 7, 1):
         a_copy(d).start()
     keep.start()
 
@@ -360,7 +360,7 @@
     def leaves(d):
         return column(d)[1] != y
 
-    for d in (0, 1, 2, 6, 3, 7, 4, 5):
+    for d in (0, 1, 2, 4, 6, 3, 5, 7):
         if d == 0:
             keep.wait()
         else:

time: 164 us -> 160 us (0.976)
  Pallas kernels: 163 us -> 158 us
    pallas_call x1, Pallas kernels: 115 us -> 111 us  [band_depth(): pl.pallas_call(band_kernel, out_shape=(jax.ShapeDtypeStruct((16, ROWS, 12...]
where the time goes in v6:
time: 160 us
  Pallas kernels  158 us (99%)
    pallas_call x1, Pallas kernels, band_depth(): pl.pallas_call(band_kernel, out_shape=(jax.ShapeDtypeStruct((16, ROWS, 12...  111 us
    pallas_call x1, Pallas kernels, share(): pl.pallas_call(share_kernel, out_shape=(jax.ShapeDtypeStruct((SEGS, 32, W...  38 us
    pallas_call x1, Pallas kernels, sightline_order(): pl.pallas_call(order_kernel, out_shape=(jax.ShapeDtypeStruct((2, ROWS), j...  7.41 us

profile of v6, /device:TPU:1, one launch (start us, length us, event | category | flops | bytes accessed | tf_op | source)
XLA Modules:
  0.0 159.8 jit_solution(14388467085914702865)
XLA Ops:
  0.0 0.0 copy-start.1
  0.0 0.7 copy-done.1
  0.7 0.0 copy-start
  0.7 0.7 copy-done
  1.4 7.4 %order.1 = (s32[2,128]{1,0:T(2,128)S(1)}, f32[16,128,128]{2,1,0:T(8,128)S(1)}, f32[16,128,128]{2,1,0:T(8,128)S(1)}, f32[16,128,128]{2,1,0:T(8,128)S(1)}) custom-call(s32[32]{0:T(128)S(1)} %copy-done.1, s32[32,32]{1,0:T(8,128)S(1)} %copy-done, f32[128,2048]{1,0:T(8,128)} %bitcast.3, f32[128,2048]{1,0:T(8,128)} %bitcast.4, f32[128,2048]{1,0:T(8,128)} %bitcast.5), custom_call_target="tpu_custom_call" | custom-call | tf_op jit(solution)/shard_map/order/pallas_call | solution.py:83
  8.8 111.1 %band.1 = (f32[16,128,128]{2,1,0:T(8,128)S(1)}, f32[16,128,128]{2,1,0:T(8,128)S(1)}) custom-call(s32[2,128]{1,0:T(2,128)S(1)} %get-tuple-element.13.table, f32[16,128,128]{2,1,0:T(8,128)S(1)} %get-tuple-element.14.d_ref, f32[16,128,128]{2,1,0:T(8,128)S(1)} %get-tuple-element.15.t_ref, f32[16,128,128]{2,1,0:T(8,128)S(1)} %get-tuple-element.16.v_ref), custom_call_target="tpu_custom_call" | custom-call | tf_op jit(solution)/shard_map/band/pallas_call | solution.py:230
  119.9 38.0 %share.1 = (f32[32,32,256]{2,1,0:T(8,128)S(1)}, f32[8,128]{1,0:T(8,128)S(1)}) custom-call(f32[16,128,128]{2,1,0:T(8,128)S(1)} %get-tuple-element.17.tau, f32[16,128,128]{2,1,0:T(8,128)S(1)} %get-tuple-element.18.edge), custom_call_target="tpu_custom_call" | custom-call | tf_op jit(solution)/shard_map/share/pallas_call | solution.py:420
  157.9 1.9 %finish.1 = f32[32,32,256]{2,1,0:T(8,128)} custom-call(s32[32]{0:T(128)S(1)} %copy-done.1, f32[32,32,256]{2,1,0:T(8,128)S(1)} %get-tuple-element.19.got, f32[8,128]{1,0:T(8,128)S(1)} %get-tuple-element.20.sums), custom_call_target="tpu_custom_call" | custom-call | tf_op jit(solution)/shard_map/finish/pallas_call | solution.py:465
Async XLA Ops:
  0.0 0.7 copy-start.1
  0.7 0.7 copy-start

commit v7 on v6

--- a/solution.py
+++ b/solution.py
@@ -145,10 +145,12 @@
         def place(dst, sk):
             shift = lax.rem(sk + 128, 128)
             inside = jnp.logical_and(lane >= sk, lane < sk + 128)
+            outside = jnp.logical_not(inside)
             for r in range(16):
                 z = pltpu.roll(Zb[1 - dst, r], shift, 1)
-                S[base + r] = S[base + r] + jnp.where(inside, z, 0.0)
-                E[base + r] = E[base + r] + jnp.where(inside, 0.0, z)
+                both = jnp.where(inside, S[base + r], E[base + r]) + z
+                pltpu.store(S.at[base + r], both, mask=inside)
+                pltpu.store(E.at[base + r], both, mask=outside)
 
         def cells(Z, kf, masked):
             for s in range(16):

time: 160 us -> 162 us (1.012)
  Pallas kernels: 158 us -> 161 us
    pallas_call x1, Pallas kernels: 111 us -> 114 us  [band_depth(): pl.pallas_call(band_kernel, out_shape=(jax.ShapeDtypeStruct((16, ROWS, 12...]
where the time goes in v7:
time: 162 us; the launch traced here: 163 us
  Pallas kernels  161 us (99%)
    pallas_call x1, Pallas kernels, band_depth(): pl.pallas_call(band_kernel, out_shape=(jax.ShapeDtypeStruct((16, ROWS, 12...  114 us
    pallas_call x1, Pallas kernels, share(): pl.pallas_call(share_kernel, out_shape=(jax.ShapeDtypeStruct((SEGS, 32, W...  38.5 us
    pallas_call x1, Pallas kernels, sightline_order(): pl.pallas_call(order_kernel, out_shape=(jax.ShapeDtypeStruct((2, ROWS), j...  7.41 us

profile of v7, /device:TPU:1, one launch (start us, length us, event | category | flops | bytes accessed | tf_op | source)
XLA Modules:
  0.0 162.7 jit_solution(6946285932146501187)
XLA Ops:
  0.0 0.0 copy-start.1
  0.0 0.7 copy-done.1
  0.7 0.0 copy-start
  0.7 0.7 copy-done
  1.4 7.4 %order.1 = (s32[2,128]{1,0:T(2,128)S(1)}, f32[16,128,128]{2,1,0:T(8,128)S(1)}, f32[16,128,128]{2,1,0:T(8,128)S(1)}, f32[16,128,128]{2,1,0:T(8,128)S(1)}) custom-call(s32[32]{0:T(128)S(1)} %copy-done.1, s32[32,32]{1,0:T(8,128)S(1)} %copy-done, f32[128,2048]{1,0:T(8,128)} %bitcast.3, f32[128,2048]{1,0:T(8,128)} %bitcast.4, f32[128,2048]{1,0:T(8,128)} %bitcast.5), custom_call_target="tpu_custom_call" | custom-call | tf_op jit(solution)/shard_map/order/pallas_call | solution.py:83
  8.8 113.5 %band.1 = (f32[16,128,128]{2,1,0:T(8,128)S(1)}, f32[16,128,128]{2,1,0:T(8,128)S(1)}) custom-call(s32[2,128]{1,0:T(2,128)S(1)} %get-tuple-element.13.table, f32[16,128,128]{2,1,0:T(8,128)S(1)} %get-tuple-element.14.d_ref, f32[16,128,128]{2,1,0:T(8,128)S(1)} %get-tuple-element.15.t_ref, f32[16,128,128]{2,1,0:T(8,128)S(1)} %get-tuple-element.16.v_ref), custom_call_target="tpu_custom_call" | custom-call | tf_op jit(solution)/shard_map/band/pallas_call | solution.py:232
  122.3 38.5 %share.1 = (f32[32,32,256]{2,1,0:T(8,128)S(1)}, f32[8,128]{1,0:T(8,128)S(1)}) custom-call(f32[16,128,128]{2,1,0:T(8,128)S(1)} %get-tuple-element.17.tau, f32[16,128,128]{2,1,0:T(8,128)S(1)} %get-tuple-element.18.edge), custom_call_target="tpu_custom_call" | custom-call | tf_op jit(solution)/shard_map/share/pallas_call | solution.py:422
  160.9 1.9 %finish.1 = f32[32,32,256]{2,1,0:T(8,128)} custom-call(s32[32]{0:T(128)S(1)} %copy-done.1, f32[32,32,256]{2,1,0:T(8,128)S(1)} %get-tuple-element.19.got, f32[8,128]{1,0:T(8,128)S(1)} %get-tuple-element.20.sums), custom_call_target="tpu_custom_call" | custom-call | tf_op jit(solution)/shard_map/finish/pallas_call | solution.py:467
Async XLA Ops:
  0.0 0.7 copy-start.1
  0.7 0.7 copy-start
